TPU v7x, 32 devices: a whole 2x2x4 slice. The times are simulated.
32 devices in a mesh: dp: 4 (over y, x), ctx: 8 (over z, core).
Axes of the slice: x: 2, y: 2, z: 4, core: 2. Of those that a mesh axis runs over, the one named last changes fastest.
Arguments:
- inputs: bfloat16 [8, 512, 1536], P('dp', 'ctx'), may hold values from -6 to 6
- cotangent: bfloat16 [8, 512, 1536], P('dp', 'ctx'), may hold values from -6 to 6
- query_weight: bfloat16 [1536, 1536], P(('dp', 'ctx')), may hold values from -0.15625 to 0.15625
- key_weight: bfloat16 [1536, 768], P(('dp', 'ctx')), may hold values from -0.15625 to 0.15625
- value_weight: bfloat16 [1536, 768], P(('dp', 'ctx')), may hold values from -0.15625 to 0.15625
- output_weight: bfloat16 [1536, 1536], P(('dp', 'ctx')), may hold values from -2.5 to 2.5
- attn_gain: bfloat16 [1536], P(('dp', 'ctx')), may hold values from 0.25 to 1.75
- gate_weight: bfloat16 [1536, 4096], P(('dp', 'ctx')), may hold values from -0.15625 to 0.15625
- up_weight: bfloat16 [1536, 4096], P(('dp', 'ctx')), may hold values from -0.15625 to 0.15625
- down_weight: bfloat16 [4096, 1536], P(('dp', 'ctx')), may hold values from -0.09375 to 0.09375
- mlp_gain: bfloat16 [1536], P(('dp', 'ctx')), may hold values from 0.25 to 1.75
Outputs:
- layer_out: bfloat16 [8, 512, 1536], P('dp', 'ctx')
- inputs_grad: bfloat16 [8, 512, 1536], P('dp', 'ctx')
- query_grad: float32 [1536, 1536], P(('dp', 'ctx'))
- key_grad: float32 [1536, 768], P(('dp', 'ctx'))
- value_grad: float32 [1536, 768], P(('dp', 'ctx'))
- output_grad: float32 [1536, 1536], P(('dp', 'ctx'))
- attn_gain_grad: float32 [1536], P(('dp', 'ctx'))
- gate_grad: float32 [1536, 4096], P(('dp', 'ctx'))
- up_grad: float32 [1536, 4096], P(('dp', 'ctx'))
- down_grad: float32 [4096, 1536], P(('dp', 'ctx'))
- mlp_gain_grad: float32 [1536], P(('dp', 'ctx'))
All inputs are finite; a program needn't handle non-finite values.
Results may differ from a plain program's by a relative error of at most 0.014.
Values may be sent and summed in bfloat16 or wider, within the bound.
No kernel may reach another device: no remote copies, remote signals or barrier semaphores. Data moves between devices by JAX's collectives and lax.ppermute only.
A program may use at most 320 MiB of HBM per device.

v0:
```python
import jax
import jax.numpy as jnp
from jax import lax
from jax.sharding import PartitionSpec as P

HEADS = 16
KV_HEADS = 8
HEAD_DIM = 96


epsilon = 1e-05
rope_base = 100000.0


def angles(row_count, start_pos, head_dim):
    half_dim = head_dim // 2
    positions = (start_pos + jnp.arange(row_count, dtype=jnp.int32)).astype(jnp.float32)
    frequency = rope_base ** (-(2.0 * jnp.arange(half_dim, dtype=jnp.float32)) / head_dim)
    angle_table = positions[:, None] * frequency[None, :]
    return (jnp.cos(angle_table), jnp.sin(angle_table))


def rotate(field, cosine, sine_table, head_dim, inverse):
    field_shape = field.shape
    split_heads = field.reshape(field_shape[:-1] + (field_shape[-1] // head_dim, head_dim))
    half_dim = head_dim // 2
    first_half = split_heads[..., :half_dim]
    second_half = split_heads[..., half_dim:]
    cos_part = cosine[:, None, :]
    sin_part = sine_table[:, None, :]
    if inverse:
        rotated = jnp.concatenate(
            [
                first_half * cos_part + second_half * sin_part,
                second_half * cos_part - first_half * sin_part,
            ],
            -1,
        )
    else:
        rotated = jnp.concatenate(
            [
                first_half * cos_part - second_half * sin_part,
                second_half * cos_part + first_half * sin_part,
            ],
            -1,
        )
    return rotated.reshape(field_shape)


def body(
    inputs,
    cotangent,
    query_weight,
    key_weight,
    value_weight,
    output_weight,
    attn_gain,
    gate_weight,
    up_weight,
    down_weight,
    mlp_gain,
):
    seq_here, span_rows, model_width = inputs.shape
    token_rows = seq_here * span_rows
    ctx_rank = lax.axis_index("ctx")
    kv_width = KV_HEADS * HEAD_DIM
    group_size = HEADS // KV_HEADS
    group_width = group_size * HEAD_DIM
    score_scale = HEAD_DIM ** (-0.5)
    attn_full = (
        lax.all_gather(query_weight, ("dp", "ctx"), axis=0, tiled=True),
        lax.all_gather(key_weight, ("dp", "ctx"), axis=0, tiled=True),
        lax.all_gather(value_weight, ("dp", "ctx"), axis=0, tiled=True),
        lax.all_gather(output_weight, ("dp", "ctx"), axis=0, tiled=True),
        lax.all_gather(attn_gain, ("dp", "ctx"), axis=0, tiled=True),
    )
    query_full, key_full, value_full, output_full, attn_gain_full = attn_full
    input_widened = inputs.astype(jnp.float32).reshape(token_rows, model_width)
    recip_one = lax.rsqrt(jnp.mean(input_widened * input_widened, -1, keepdims=True) + epsilon)
    normed_one = (input_widened * recip_one * attn_gain_full.astype(jnp.float32)).astype(
        jnp.bfloat16
    )
    query_raw = jnp.dot(normed_one, query_full, preferred_element_type=jnp.float32)
    key_raw = jnp.dot(normed_one, key_full, preferred_element_type=jnp.float32)
    value_raw = jnp.dot(normed_one, value_full, preferred_element_type=jnp.float32)
    cosine, sine_table = angles(span_rows, ctx_rank * span_rows, HEAD_DIM)
    queries = (
        rotate(query_raw.reshape(seq_here, span_rows, -1), cosine, sine_table, HEAD_DIM, False)
        * score_scale
    ).astype(jnp.bfloat16)
    keys_rot = rotate(
        key_raw.reshape(seq_here, span_rows, -1), cosine, sine_table, HEAD_DIM, False
    ).astype(jnp.bfloat16)
    values_low = value_raw.reshape(seq_here, span_rows, kv_width).astype(jnp.bfloat16)
    kv_local = jnp.concatenate([keys_rot, values_low], -1)
    kv_all = lax.all_gather(kv_local, "ctx", axis=1, tiled=True)
    seq_length = kv_all.shape[1]
    query_place = ctx_rank * span_rows + jnp.arange(span_rows, dtype=jnp.int32)
    key_place = jnp.arange(seq_length, dtype=jnp.int32)
    allowed = key_place[None, :] <= query_place[:, None]

    def group_slice(source, kv_head):
        piece = lax.dynamic_slice_in_dim(source, kv_head * group_width, group_width, 2)
        return piece.reshape(seq_here, span_rows, group_size, HEAD_DIM)

    def head_parts(kv_source, kv_head):
        key_portion = lax.dynamic_slice_in_dim(kv_source, kv_head * HEAD_DIM, HEAD_DIM, 2)
        value_portion = lax.dynamic_slice_in_dim(
            kv_source, kv_width + kv_head * HEAD_DIM, HEAD_DIM, 2
        )
        return (key_portion, value_portion)

    def masked_scores(query_portion, key_portion):
        scores = jnp.einsum(
            "awuh,afh->auwf", query_portion, key_portion, preferred_element_type=jnp.float32
        )
        return jnp.where(allowed[None, None], scores, -1e30)

    def forward_head(attended, kv_head):
        query_portion = group_slice(queries, kv_head)
        key_portion, value_portion = head_parts(kv_all, kv_head)
        scores = masked_scores(query_portion, key_portion)
        highest_score = jnp.max(scores, -1, keepdims=True)
        log_total = highest_score + jnp.log(
            jnp.sum(jnp.exp(scores - highest_score), -1, keepdims=True)
        )
        probability_reduced = jnp.exp(scores - log_total).astype(jnp.bfloat16)
        head_out = jnp.einsum(
            "obzf,ofp->ozbp", probability_reduced, value_portion, preferred_element_type=jnp.float32
        )
        attended = lax.dynamic_update_slice_in_dim(
            attended, head_out.reshape(seq_here, span_rows, group_width), kv_head * group_width, 2
        )
        return (attended, log_total)

    head_ids = jnp.arange(KV_HEADS, dtype=jnp.int32)
    attended_work, log_totals = lax.scan(
        forward_head, jnp.zeros((seq_here, span_rows, HEADS * HEAD_DIM), jnp.float32), head_ids
    )
    attended_work_low = attended_work.astype(jnp.bfloat16)
    attended_low = attended_work_low.reshape(token_rows, -1)
    residual = input_widened + jnp.dot(
        attended_low, output_full, preferred_element_type=jnp.float32
    )
    mlp_full = (
        lax.all_gather(gate_weight, ("dp", "ctx"), axis=0, tiled=True),
        lax.all_gather(up_weight, ("dp", "ctx"), axis=0, tiled=True),
        lax.all_gather(down_weight, ("dp", "ctx"), axis=0, tiled=True),
        lax.all_gather(mlp_gain, ("dp", "ctx"), axis=0, tiled=True),
    )
    gate_full, up_full, down_full, mlp_gain_full = mlp_full
    recip_two = lax.rsqrt(jnp.mean(residual * residual, -1, keepdims=True) + epsilon)
    normed_two = (residual * recip_two * mlp_gain_full.astype(jnp.float32)).astype(jnp.bfloat16)
    gate_act = jnp.dot(normed_two, gate_full, preferred_element_type=jnp.float32)
    up_act = jnp.dot(normed_two, up_full, preferred_element_type=jnp.float32)
    sigmoid_gate = jax.nn.sigmoid(gate_act)
    silu_gate = gate_act * sigmoid_gate
    hidden_low = (silu_gate * up_act).astype(jnp.bfloat16)
    layer_out = (
        (residual + jnp.dot(hidden_low, down_full, preferred_element_type=jnp.float32))
        .astype(jnp.bfloat16)
        .reshape(inputs.shape)
    )
    back_mlp = (
        lax.all_gather(gate_weight, ("dp", "ctx"), axis=0, tiled=True),
        lax.all_gather(up_weight, ("dp", "ctx"), axis=0, tiled=True),
        lax.all_gather(down_weight, ("dp", "ctx"), axis=0, tiled=True),
        lax.all_gather(mlp_gain, ("dp", "ctx"), axis=0, tiled=True),
    )
    back_attn = (
        lax.all_gather(query_weight, ("dp", "ctx"), axis=0, tiled=True),
        lax.all_gather(key_weight, ("dp", "ctx"), axis=0, tiled=True),
        lax.all_gather(value_weight, ("dp", "ctx"), axis=0, tiled=True),
        lax.all_gather(output_weight, ("dp", "ctx"), axis=0, tiled=True),
        lax.all_gather(attn_gain, ("dp", "ctx"), axis=0, tiled=True),
    )
    gate_back, up_back, down_back, mlp_gain_back = back_mlp
    query_back, key_back, value_back, output_back, attn_gain_back = back_attn
    grad_out = cotangent.reshape(token_rows, model_width)
    grad_hidden = jnp.einsum("nd,fd->nf", grad_out, down_back, preferred_element_type=jnp.float32)
    grad_gate = (
        grad_hidden * up_act * sigmoid_gate * (1.0 + gate_act * (1.0 - sigmoid_gate))
    ).astype(jnp.bfloat16)
    grad_up = (grad_hidden * silu_gate).astype(jnp.bfloat16)
    grad_two = jnp.einsum(
        "nf,df->nd", grad_gate, gate_back, preferred_element_type=jnp.float32
    ) + jnp.einsum("nf,df->nd", grad_up, up_back, preferred_element_type=jnp.float32)
    scaled_two = grad_two * mlp_gain_back.astype(jnp.float32)
    mlp_gain_term = jnp.sum(grad_two * residual * recip_two, 0)
    grad_residual = (
        grad_out.astype(jnp.float32)
        + recip_two * scaled_two
        - residual * recip_two**3 * jnp.mean(scaled_two * residual, -1, keepdims=True)
    )
    down_grad = lax.psum_scatter(
        jnp.einsum("nf,nd->fd", hidden_low, grad_out, preferred_element_type=jnp.float32),
        ("dp", "ctx"),
        scatter_dimension=0,
        tiled=True,
    )
    grad_branch = grad_residual.astype(jnp.bfloat16)
    grad_attended = (
        jnp.einsum("nd,kd->nk", grad_branch, output_back, preferred_element_type=jnp.float32)
        .astype(jnp.bfloat16)
        .reshape(seq_here, span_rows, -1)
    )
    kv_back = lax.all_gather(kv_local, "ctx", axis=1, tiled=True)

    def backward_head(carry, head_pair):
        grad_queries, grad_kv = carry
        kv_head, log_total = head_pair
        query_portion = group_slice(queries, kv_head)
        gradient_portion = group_slice(grad_attended, kv_head)
        key_portion, value_portion = head_parts(kv_back, kv_head)
        scores = masked_scores(query_portion, key_portion)
        probs = jnp.exp(scores - log_total)
        probability_reduced = probs.astype(jnp.bfloat16)
        grad_probs = jnp.einsum(
            "awuh,afh->auwf", gradient_portion, value_portion, preferred_element_type=jnp.float32
        )
        weighted = jnp.sum(probs * grad_probs, -1, keepdims=True)
        score_gradient = (probs * (grad_probs - weighted)).astype(jnp.bfloat16)
        query_fragment = jnp.einsum(
            "obzf,ofp->ozbp", score_gradient, key_portion, preferred_element_type=jnp.float32
        )
        key_piece = jnp.einsum(
            "abfq,afbi->aqi", score_gradient, query_portion, preferred_element_type=jnp.float32
        )
        value_piece = jnp.einsum(
            "abfq,afbi->aqi",
            probability_reduced,
            gradient_portion,
            preferred_element_type=jnp.float32,
        )
        grad_queries = lax.dynamic_update_slice_in_dim(
            grad_queries,
            query_fragment.reshape(seq_here, span_rows, group_width),
            kv_head * group_width,
            2,
        )
        grad_kv = lax.dynamic_update_slice_in_dim(grad_kv, key_piece, kv_head * HEAD_DIM, 2)
        grad_kv = lax.dynamic_update_slice_in_dim(
            grad_kv, value_piece, kv_width + kv_head * HEAD_DIM, 2
        )
        return ((grad_queries, grad_kv), None)

    start_carry = (
        jnp.zeros((seq_here, span_rows, HEADS * HEAD_DIM), jnp.float32),
        jnp.zeros((seq_here, seq_length, 2 * kv_width), jnp.float32),
    )
    (grad_queries_work, grad_kv), unused = lax.scan(
        backward_head, start_carry, (head_ids, log_totals)
    )
    grad_queries = grad_queries_work
    kv_grad = lax.psum_scatter(grad_kv, "ctx", scatter_dimension=1, tiled=True)
    grad_q = (
        rotate(grad_queries * score_scale, cosine, sine_table, HEAD_DIM, True)
        .astype(jnp.bfloat16)
        .reshape(token_rows, -1)
    )
    grad_k = (
        rotate(kv_grad[..., :kv_width], cosine, sine_table, HEAD_DIM, True)
        .astype(jnp.bfloat16)
        .reshape(token_rows, -1)
    )
    grad_v = kv_grad[..., kv_width:].astype(jnp.bfloat16).reshape(token_rows, -1)
    grad_one = jnp.einsum("nk,dk->nd", grad_q, query_back, preferred_element_type=jnp.float32)
    grad_one = grad_one + jnp.einsum(
        "nk,dk->nd", grad_k, key_back, preferred_element_type=jnp.float32
    )
    grad_one = grad_one + jnp.einsum(
        "nk,dk->nd", grad_v, value_back, preferred_element_type=jnp.float32
    )
    scaled_one = grad_one * attn_gain_back.astype(jnp.float32)
    attn_gain_term = jnp.sum(grad_one * input_widened * recip_one, 0)
    inputs_grad = (
        (
            grad_residual
            + recip_one * scaled_one
            - input_widened * recip_one**3 * jnp.mean(scaled_one * input_widened, -1, keepdims=True)
        )
        .astype(jnp.bfloat16)
        .reshape(inputs.shape)
    )
    grad_projected = jnp.concatenate([grad_q, grad_k, grad_v], -1)
    grad_mlp_in = jnp.concatenate([grad_gate, grad_up], -1)
    projected_term = jnp.einsum(
        "nd,nk->dk", normed_one, grad_projected, preferred_element_type=jnp.float32
    )
    output_term = jnp.einsum(
        "nk,nd->kd", attended_low, grad_branch, preferred_element_type=jnp.float32
    )
    mlp_term = jnp.einsum("nd,nf->df", normed_two, grad_mlp_in, preferred_element_type=jnp.float32)
    row_grad = lax.psum_scatter(
        jnp.concatenate([projected_term, output_term, mlp_term], 1),
        ("dp", "ctx"),
        scatter_dimension=0,
        tiled=True,
    )
    gain_grad = lax.psum_scatter(
        jnp.stack([attn_gain_term, mlp_gain_term]), ("dp", "ctx"), scatter_dimension=1, tiled=True
    )
    q_width = HEADS * HEAD_DIM
    value_start = q_width + kv_width
    output_start = value_start + kv_width
    gate_start = output_start + model_width
    ff_width = gate_back.shape[1]
    up_start = gate_start + ff_width
    query_grad = row_grad[:, :q_width]
    key_grad = row_grad[:, q_width:value_start]
    value_grad = row_grad[:, value_start:output_start]
    output_grad = row_grad[:, output_start:gate_start]
    gate_grad = row_grad[:, gate_start:up_start]
    up_grad = row_grad[:, up_start : up_start + ff_width]
    return (
        layer_out,
        inputs_grad,
        query_grad,
        key_grad,
        value_grad,
        output_grad,
        gain_grad[0],
        gate_grad,
        up_grad,
        down_grad,
        gain_grad[1],
    )


def solution(mesh):
    placed = (
        P("dp", "ctx", None),
        P("dp", "ctx", None),
        P(("dp", "ctx"), None),
        P(("dp", "ctx"), None),
        P(("dp", "ctx"), None),
        P(("dp", "ctx"), None),
        P(("dp", "ctx")),
        P(("dp", "ctx"), None),
        P(("dp", "ctx"), None),
        P(("dp", "ctx"), None),
        P(("dp", "ctx")),
    )
    return jax.shard_map(
        body,
        mesh=mesh,
        in_specs=placed,
        out_specs=(
            P("dp", "ctx", None),
            P("dp", "ctx", None),
            P(("dp", "ctx"), None),
            P(("dp", "ctx"), None),
            P(("dp", "ctx"), None),
            P(("dp", "ctx"), None),
            P(("dp", "ctx")),
            P(("dp", "ctx"), None),
            P(("dp", "ctx"), None),
            P(("dp", "ctx"), None),
            P(("dp", "ctx")),
        ),
        check_vma=False,
    )
```

profile of v0, /device:TPU:0, one launch (start us, length us, event | category | flops | bytes accessed | tf_op | source)
XLA Modules:
  0.0 1836.6 jit_solution(15092728423978344488)
XLA Ops:
  11.2 42.1 %all-reduce.2 = (bf16[1536]{0:T(1024)(128)(2,1)S(1)}, bf16[1536]{0:T(1024)(128)(2,1)S(1)}) all-reduce(bf16[1536]{0:T(1024)(128)(2,1)S(1)} %dynamic-update-slice, bf16[1536]{0:T(1024)(128)(2,1)S(1)} %dynamic-update-slice.1), channel_id=1, replica_groups=mesh['dp'=4,'ctx'=8] {'dp','ctx'}, use_global_device_ids=true, to_apply=%add | all-reduce | flops 3072 | bytes 12288
  54.7 16.2 all-gather.9.cloned.1.call-done
  70.9 4.3 copy.55
  75.2 2.7 fusion.63
  78.7 51.2 %all-gather.11.cloned.1.call-done = bf16[1536,768]{1,0:T(8,128)(2,1)} async-done(((bf16[48,768]{1,0:T(8,128)(2,1)}), bf16[1536,768]{1,0:T(8,128)(2,1)}) %all-gather.11.cloned.1.call-update) | async-done | bytes 2359312 | tf_op jit(solution)/shard_map/all_gather | solution.py:73
  129.9 2.2 fusion.40
  135.7 59.7 %all-gather.15.cloned.1.call-done = bf16[1536,1536]{1,0:T(8,128)(2,1)} async-done(((bf16[48,1536]{1,0:T(8,128)(2,1)}), bf16[1536,1536]{1,0:T(8,128)(2,1)}) %all-gather.15.cloned.1.call-update) | async-done | bytes 4718608 | tf_op jit(solution)/shard_map/all_gather | solution.py:71
  195.4 6.7 copy.57
  202.0 4.7 fusion.61
  209.3 24.7 %all-gather.13.cloned.1.call-done = bf16[2,512,1536]{2,1,0:T(8,128)(2,1)} async-done(((bf16[2,64,1536]{2,1,0:T(8,128)(2,1)}), bf16[2,512,1536]{2,1,0:T(8,128)(2,1)}) %all-gather.13.cloned.1.call-update) | async-done | bytes 3145744 | tf_op jit(solution)/shard_map/all_gather | solution.py:96
  234.0 4.7 copy.59
  238.7 58.0 %while.30 = (s32[]{:T(128)}, bf16[2,64,1536]{2,1,0:T(8,128)(2,1)S(1)}, f32[8,2,2,64,1]{3,2,1,4,0:T(2,128)}, s32[8]{0:T(128)S(1)}, bf16[2,512,1536]{1,2,0:T(8,128...) while((s32[]{:T(128)}, ...), condition=%wide.region_4.5_spmd.clone, body=%wide.region_1.4_spmd.clone.sunk | while | flops 51150600 | bytes 2631223 | solution.py:137
  296.6 2.8 all-gather.17.cloned.1.call-done
  299.4 3.2 multiply_reduce_fusion.3
  302.8 93.1 %all-gather.21.cloned.1.call-done = bf16[1536,4096]{1,0:T(8,128)(2,1)} async-done(((bf16[48,4096]{1,0:T(8,128)(2,1)}), bf16[1536,4096]{1,0:T(8,128)(2,1)}) %all-gather.21.cloned.1.call-update) | async-done | bytes 12582928 | tf_op jit(solution)/shard_map/all_gather | solution.py:147
  395.9 7.8 fusion.82
  403.7 89.1 %all-gather.19.cloned.1.call-done = bf16[1536,4096]{1,0:T(8,128)(2,1)} async-done(((bf16[48,4096]{1,0:T(8,128)(2,1)}), bf16[1536,4096]{1,0:T(8,128)(2,1)}) %all-gather.19.cloned.1.call-update) | async-done | bytes 12582928 | tf_op jit(solution)/shard_map/all_gather | solution.py:146
  492.8 7.8 fusion.81
  500.5 89.1 %all-gather.23.cloned.1.call-done = bf16[4096,1536]{1,0:T(8,128)(2,1)} async-done(((bf16[128,1536]{1,0:T(8,128)(2,1)}), bf16[4096,1536]{1,0:T(8,128)(2,1)}) %all-gather.23.cloned.1.call-update) | async-done | bytes 12582928 | tf_op jit(solution)/shard_map/all_gather | solution.py:148
  589.7 11.2 multiply_convert_fusion.1
  600.9 9.6 fusion.83
  610.6 9.8 multiply_reduce_fusion.1
  620.7 2.4 convolution_convert_fusion
  624.1 3.4 broadcast_in_dim.58
  627.4 93.6 %while.31 = (s32[]{:T(128)}, f32[2,64,1536]{2,1,0:T(8,128)}, f32[2,512,1536]{1,2,0:T(8,128)}, s32[8]{0:T(128)S(1)}, bf16[2,512,1536]{1,2,0:T(8,128)(2,1)}, /*ind...) while((s32[]{:T(128)}, f32[2,64,1536]{2,1,0:T(8,128)}, ...), condition=%wide.region_9.10_spmd.clone, body=%wide.region_7.9_spmd.clone.sunk | while | flops 126910224 | bytes 6657619 | solution.py:251
  646.9 2.0 dynamic_update_slice.48
  670.4 2.0 dynamic_update_slice.48
  693.9 2.0 dynamic_update_slice.48
  717.2 1.8 dynamic_update_slice.48
  721.0 6.6 copy.64
  731.4 2.4 fusion.78
  737.6 5.0 fusion.84
  742.6 5.0 fusion.68
  747.7 21.7 %fusion.35 = f32[1536,8192]{1,0:T(8,128)} fusion(bf16[128,1536]{1,0:T(8,128)(2,1)S(1)} %multiply_convert_fusion.4, bf16[128,4096]{1,0:T(8,128)(2,1)} %copy-done.4, bf16[128,4096]{1,0:T(8,128)(2,1)} %copy-done.5), kind=kOutput, calls=%fused_computation.59 | convolution fusion | flops 3225419776 | bytes 52822016 | tf_op jit(solution)/shard_map/nd,nf->df/dot_general | solution.py:293
  769.4 26.7 %reduce-scatter.7.cloned.1.call-done = f32[2,64,1536]{2,1,0:T(8,128)} async-done(((f32[2,512,1536]{2,1,0:T(8,128)}), f32[2,64,1536]{2,1,0:T(8,128)}) %reduce-scatter.7.cloned.1.call-update) | async-done | bytes 786448 | tf_op jit(solution)/shard_map/reduce_scatter | solution.py:255
  799.6 2.8 convolution_add_fusion.1
  802.4 2.2 fusion.60
  805.3 1.9 copy.77
  807.2 9.0 fusion.44
  816.3 52.3 %pad_maximum_fusion = f32[1536,12800]{1,0:T(8,128)} fusion(f32[1536,8192]{1,0:T(8,128)} %fusion.35, f32[1536,1536]{1,0:T(8,128)} %fusion.68, f32[1536,3072]{1,0:T(8,128)} %fusion.44), kind=kLoop, calls=%fused_computation.49 | loop fusion | flops 39321600 | bytes 157286400 | tf_op jit(solution)/shard_map/concatenate | solution.py:295
  869.5 11.5 fusion.85
  881.7 7.5 fusion.32
  890.3 11.7 reduce-scatter.13.cloned.1.call-done
  904.0 676.1 %reduce-scatter.9.cloned.1.call-done = f32[48,12800]{1,0:T(8,128)} async-done(((f32[1536,12800]{1,0:T(8,128)}), f32[48,12800]{1,0:T(8,128)}) %reduce-scatter.9.cloned.1.call-update) | async-done | bytes 2457616 | tf_op jit(solution)/shard_map/reduce_scatter | solution.py:294
  1580.1 1.7 fusion.77
  1581.8 1.9 fusion.76
  1583.7 2.6 fusion.75
  1586.3 242.9 %reduce-scatter.11.cloned.1.call-done = f32[128,1536]{1,0:T(8,128)} async-done(((f32[4096,1536]{1,0:T(8,128)}), f32[128,1536]{1,0:T(8,128)}) %reduce-scatter.11.cloned.1.call-update) | async-done | bytes 786448 | tf_op jit(solution)/shard_map/reduce_scatter | solution.py:195
  (337 shorter events, 151.5 us)
Async XLA Ops:
  7.2 68.0 %copy-start = (bf16[2,64,1536]{2,1,0:T(8,128)(2,1)S(1)}, bf16[2,64,1536]{2,1,0:T(8,128)(2,1)}, u32[]{:S(2)}) copy-start(bf16[2,64,1536]{2,1,0:T(8,128)(2,1)} %param.15) | copy-start | bytes 1179652
  7.2 63.7 %all-gather.9.cloned.1.call-start = ((), (), s32[]{:S(2)}) async-start(), calls=%async_computation.4 | async-start | bytes 2433024 | tf_op jit(solution)/shard_map/all_gather | solution.py:72
  7.9 122.0 %all-gather.11.cloned.1.call-start = ((), (), s32[]{:S(2)}) async-start(), calls=%async_computation.5 | async-start | bytes 2433024 | tf_op jit(solution)/shard_map/all_gather | solution.py:73
  8.7 186.7 %all-gather.15.cloned.1.call-start = ((), (), s32[]{:S(2)}) async-start(), calls=%async_computation.7 | async-start | bytes 4866048 | tf_op jit(solution)/shard_map/all_gather | solution.py:71
  9.4 224.6 %all-gather.13.cloned.1.call-start = ((), (), s32[]{:S(2)}) async-start(), calls=%async_computation.6 | async-start | bytes 3538944 | tf_op jit(solution)/shard_map/all_gather | solution.py:96
  54.5 147.6 %copy-start.20 = (f32[2,64]{1,0:T(2,128)}, f32[2,64]{1,0:T(2,128)S(1)}, u32[]{:S(2)}) copy-start(f32[2,64]{1,0:T(2,128)S(1)} %add_rsqrt_fusion) | copy-start | bytes 1540
  54.7 152.1 %copy-start.12 = (f32[64,48]{1,0:T(8,128)}, f32[64,48]{1,0:T(8,128)S(1)}, u32[]{:S(2)}) copy-start(f32[64,48]{1,0:T(8,128)S(1)} %get-tuple-element.375) | copy-start | bytes 36868
  54.7 152.1 %copy-start.15 = (f32[64,48]{1,0:T(8,128)}, f32[64,48]{1,0:T(8,128)S(1)}, u32[]{:S(2)}) copy-start(f32[64,48]{1,0:T(8,128)S(1)} %get-tuple-element.376) | copy-start | bytes 36868
  132.9 166.5 %all-gather.17.cloned.1.call-start = ((), (), s32[]{:S(2)}) async-start(), calls=%async_computation.8 | async-start | bytes 4866048 | tf_op jit(solution)/shard_map/all_gather | solution.py:74
  133.5 262.4 %all-gather.21.cloned.1.call-start = ((), (), s32[]{:S(2)}) async-start(), calls=%async_computation.10 | async-start | bytes 12976128 | tf_op jit(solution)/shard_map/all_gather | solution.py:147
  134.1 358.7 %all-gather.19.cloned.1.call-start = ((), (), s32[]{:S(2)}) async-start(), calls=%async_computation.9 | async-start | bytes 12976128 | tf_op jit(solution)/shard_map/all_gather | solution.py:146
  134.8 454.8 %all-gather.23.cloned.1.call-start = ((), (), s32[]{:S(2)}) async-start(), calls=%async_computation.11 | async-start | bytes 12976128 | tf_op jit(solution)/shard_map/all_gather | solution.py:148
  135.6 660.5 %reduce-scatter.7.cloned.1.call-start = ((), (), s32[]{:S(2)}) async-start(), calls=%async_computation.12 | async-start | bytes 7077888 | tf_op jit(solution)/shard_map/reduce_scatter | solution.py:255
  296.6 2.8 copy-start.18
  296.6 107.1 %copy-start.2 = (bf16[2,64,1536]{2,1,0:T(8,128)(2,1)}, bf16[2,64,1536]{2,1,0:T(8,128)(2,1)S(1)}, u32[]{:S(2)}) copy-start(bf16[2,64,1536]{2,1,0:T(8,128)(2,1)S(1)} %get-tuple-element.215) | copy-start | bytes 1179652
  492.8 96.9 %copy-start.10 = (bf16[2,64,1536]{2,1,0:T(8,128)(2,1)S(1)}, bf16[2,64,1536]{2,1,0:T(8,128)(2,1)}, u32[]{:S(2)}) copy-start(bf16[2,64,1536]{2,1,0:T(8,128)(2,1)} %param.16) | copy-start | bytes 1179652
  600.9 9.7 copy-start.5
  600.9 9.7 copy-start.4
  600.9 19.8 %slice-start = ((s8[4718592]{0:T(1024)(128)(4,1)}), s8[4194304]{0:T(1024)(128)(4,1)S(1)}, s32[]{:S(2)}) async-start(s8[4718592]{0:T(1024)(128)(4,1)} %bitcast.191), calls=%async_computation.16 | async-start | bytes 8388608
  610.6 10.1 slice-start.1
  623.1 4.3 copy-start.19
  727.6 0.7 copy-start.21
  727.6 1.3 copy-start.22
  727.6 6.2 copy-start.13
  727.6 6.2 copy-start.16
  727.6 174.3 %reduce-scatter.13.cloned.1.call-start = ((), (), s32[]{:S(2)}) async-start(), calls=%async_computation.15 | async-start | bytes 811008
  734.5 8.1 copy-start.3
  737.6 10.1 copy-start.6
  747.7 49.9 %copy-start.14 = (f32[64,48]{1,0:T(8,128)S(1)}, f32[64,48]{1,0:T(8,128)}, u32[]{:S(2)}) copy-start(f32[64,48]{1,0:T(8,128)} %copy-done.12) | copy-start | bytes 36868
  747.7 49.9 %copy-start.17 = (f32[64,48]{1,0:T(8,128)S(1)}, f32[64,48]{1,0:T(8,128)}, u32[]{:S(2)}) copy-start(f32[64,48]{1,0:T(8,128)} %copy-done.15) | copy-start | bytes 36868
  798.4 4.0 copy-start.8
  798.4 4.0 copy-start.1
  799.5 5.1 copy-start.9
  799.6 7.7 copy-start.7
  807.2 773.0 %reduce-scatter.9.cloned.1.call-start = ((), (), s32[]{:S(2)}) async-start(), calls=%async_computation.13 | async-start | bytes 81100800 | tf_op jit(solution)/shard_map/reduce_scatter | solution.py:294
  868.6 1.0 copy-start.11
  868.6 960.7 %reduce-scatter.11.cloned.1.call-start = ((), (), s32[]{:S(2)}) async-start(), calls=%async_computation.14 | async-start | bytes 25952256 | tf_op jit(solution)/shard_map/reduce_scatter | solution.py:195
  881.1 0.7 copy-start.23
  881.7 7.5 copy-start.24
Sparse Core Ops, SparseCore 0:
  11.0 59.8 all-gather.8
  73.9 55.9 all-gather.10
  132.9 62.4 all-gather.14
  197.4 36.5 all-gather.12
  236.8 62.5 all-gather.16
  302.3 93.5 all-gather.20
  398.9 93.8 all-gather.18
  495.8 93.8 all-gather.22
  727.7 68.2 reduce-scatter.6
  807.3 94.6 reduce-scatter.12
  908.4 671.6 reduce-scatter.8
  1587.0 242.2 reduce-scatter.10
where the time goes:
time: 1850 us; the launch traced here: 1840 us
  waiting for transfers between devices  1390 us (75%)
  matrix products  191 us (10%)
  local copies, waits for them, and re-layouts  109 us (6%)
  other arithmetic  69.3 us (4%)
  blocking collectives  42.1 us (2%)
  loops' own time  22.2 us (1%)
    reduce_scatter x1, waiting for transfers between devices, body(): lax.psum_scatter(jnp.concatenate([projected_term, output_term, mlp_term],...  676 us
    reduce_scatter x1, waiting for transfers between devices, body(): lax.psum_scatter(jnp.einsum('nf,nd->fd', hidden_low, grad_out, preferred_...  243 us
    all_gather x1, waiting for transfers between devices, body(): lax.all_gather(up_weight, ('dp', 'ctx'), axis=0, tiled=True)  93.1 us
    all_gather x1, waiting for transfers between devices, body(): lax.all_gather(down_weight, ('dp', 'ctx'), axis=0, tiled=True)  89.1 us
    all_gather x1, waiting for transfers between devices, body(): lax.all_gather(gate_weight, ('dp', 'ctx'), axis=0, tiled=True)  89.1 us
    all_gather x1, waiting for transfers between devices, body(): lax.all_gather(query_weight, ('dp', 'ctx'), axis=0, tiled=True)  59.7 us
    concatenate x1, other arithmetic, body(): jnp.concatenate([projected_term, output_term, mlp_term], 1)  52.3 us
    all_gather x1, waiting for transfers between devices, body(): lax.all_gather(value_weight, ('dp', 'ctx'), axis=0, tiled=True)  51.2 us
  transfers between devices with their start and end apart: 12, of which 12 were waited for; matrix products, arithmetic and copies ran while one was open for 12% of the time, Pallas kernels for 0%

commit v1 on v0

--- a/solution.py
+++ b/solution.py
@@ -1,3 +1,5 @@
+import functools
+
 import jax
 import jax.numpy as jnp
 from jax import lax
@@ -327,6 +329,221 @@
     )
 
 
+def row_norm(field):
+    return lax.rsqrt(jnp.mean(field * field, -1, keepdims=True) + epsilon)
+
+
+def gather_ctx(block):
+    return lax.all_gather(block, "ctx", axis=1, tiled=True)
+
+
+def reduce_ctx(partial):
+    return lax.psum_scatter(partial, "ctx", scatter_dimension=1, tiled=True)
+
+
+def mm(left, right, dims):
+    return jnp.einsum(dims, left, right, preferred_element_type=jnp.float32)
+
+
+def head_body(
+    dp_size,
+    inputs,
+    cotangent,
+    query_weight,
+    key_weight,
+    value_weight,
+    output_weight,
+    attn_gain,
+    gate_weight,
+    up_weight,
+    down_weight,
+    mlp_gain,
+):
+    f32, bf16 = jnp.float32, jnp.bfloat16
+    ranks = KV_HEADS
+    seq_here, span_rows, model_width = inputs.shape
+    seq_length = span_rows * ranks
+    tokens = seq_here * seq_length
+    local = seq_here * span_rows
+    weight_rows = query_weight.shape[0]
+    ff_width = gate_weight.shape[1]
+    group = HEADS // KV_HEADS
+    group_width = group * HEAD_DIM
+    head_width = group_width + 2 * HEAD_DIM
+    piece = down_weight.shape[0]
+    hidden_width = dp_size * piece
+    score_scale = HEAD_DIM ** (-0.5)
+
+    def columns(weight, width):
+        return weight.reshape(weight_rows, ranks, width)
+
+    def hidden_columns(weight):
+        split = weight.reshape(weight_rows, dp_size, ranks, piece)
+        return split.transpose(2, 0, 1, 3).reshape(ranks, weight_rows, hidden_width)
+
+    def exchange(packed):
+        return lax.all_to_all(packed, "ctx", split_axis=0, concat_axis=0, tiled=True)
+
+    head_pack = jnp.concatenate(
+        [
+            columns(query_weight, group_width),
+            columns(key_weight, HEAD_DIM),
+            columns(value_weight, HEAD_DIM),
+        ],
+        -1,
+    ).transpose(1, 0, 2)
+    head_mine = exchange(head_pack).reshape(ranks * weight_rows, head_width)
+    head_weight = lax.all_gather(head_mine, "dp", axis=0, tiled=True)
+    shards = dp_size * ranks
+    to_rank = [(i, ranks * (i % dp_size) + i // dp_size) for i in range(shards)]
+    from_rank = [(b, a) for a, b in to_rank]
+    out_mine = lax.ppermute(output_weight, ("dp", "ctx"), to_rank)
+    out_weight = lax.all_gather(out_mine, "dp", axis=0, tiled=True)
+    mlp_pack = jnp.concatenate([hidden_columns(gate_weight), hidden_columns(up_weight)], -1)
+    mlp_mine = exchange(mlp_pack).reshape(ranks * weight_rows, 2 * hidden_width)
+    mlp_weight = lax.all_gather(mlp_mine, "dp", axis=0, tiled=True)
+    down_full = lax.all_gather(down_weight, "dp", axis=0, tiled=True)
+    gains = lax.all_gather(jnp.stack([attn_gain, mlp_gain]), ("dp", "ctx"), axis=1, tiled=True)
+    attn_gain_full = gains[0].astype(f32)
+    mlp_gain_full = gains[1].astype(f32)
+
+    field = gather_ctx(inputs).astype(f32).reshape(tokens, model_width)
+    normed_one = (field * row_norm(field) * attn_gain_full).astype(bf16)
+    heads_raw = mm(normed_one, head_weight, "nd,dk->nk").reshape(seq_here, seq_length, head_width)
+    cosine, sine_table = angles(seq_length, 0, HEAD_DIM)
+    queries = (
+        rotate(heads_raw[..., :group_width], cosine, sine_table, HEAD_DIM, False) * score_scale
+    ).astype(bf16)
+    keys_rot = rotate(
+        heads_raw[..., group_width : group_width + HEAD_DIM], cosine, sine_table, HEAD_DIM, False
+    ).astype(bf16)
+    values_low = heads_raw[..., group_width + HEAD_DIM :].astype(bf16)
+    queries = queries.reshape(seq_here, seq_length, group, HEAD_DIM)
+    place = jnp.arange(seq_length, dtype=jnp.int32)
+    allowed = (place[None, :] <= place[:, None])[None, None]
+    scores = jnp.where(allowed, mm(queries, keys_rot, "sqgd,skd->sgqk"), -1e30)
+    highest_score = jnp.max(scores, -1, keepdims=True)
+    log_total = highest_score + jnp.log(
+        jnp.sum(jnp.exp(scores - highest_score), -1, keepdims=True)
+    )
+    probs = jnp.exp(scores - log_total)
+    probs_low = probs.astype(bf16)
+    attended = mm(probs_low, values_low, "sgqk,skd->sqgd").astype(bf16)
+    attended = attended.reshape(tokens, group_width)
+    branch = mm(attended, out_weight, "nk,kd->nd").astype(bf16)
+    branch = reduce_ctx(branch.reshape(seq_here, seq_length, model_width))
+    own = inputs.astype(f32).reshape(local, model_width)
+    residual = own + branch.astype(f32).reshape(local, model_width)
+    recip_two = row_norm(residual)
+    normed_two = (residual * recip_two * mlp_gain_full).astype(bf16)
+    normed_all = gather_ctx(normed_two.reshape(inputs.shape)).reshape(tokens, model_width)
+    both = mm(normed_all, mlp_weight, "nd,df->nf")
+    gate_act = both[:, :hidden_width]
+    up_act = both[:, hidden_width:]
+    sigmoid_gate = jax.nn.sigmoid(gate_act)
+    silu_gate = gate_act * sigmoid_gate
+    hidden_low = (silu_gate * up_act).astype(bf16)
+    mlp_out = mm(hidden_low, down_full, "nf,fd->nd").astype(bf16)
+    mlp_out = reduce_ctx(mlp_out.reshape(seq_here, seq_length, model_width))
+    layer_out = (residual + mlp_out.astype(f32).reshape(local, model_width)).astype(bf16)
+
+    grad_all = gather_ctx(cotangent).reshape(tokens, model_width)
+    grad_hidden = mm(grad_all, down_full, "nd,fd->nf")
+    grad_gate = (
+        grad_hidden * up_act * sigmoid_gate * (1.0 + gate_act * (1.0 - sigmoid_gate))
+    ).astype(bf16)
+    grad_up = (grad_hidden * silu_gate).astype(bf16)
+    grad_both = jnp.concatenate([grad_gate, grad_up], -1)
+    grad_two = mm(grad_both, mlp_weight, "nf,df->nd").astype(bf16)
+    grad_two = reduce_ctx(grad_two.reshape(seq_here, seq_length, model_width))
+    grad_two = grad_two.astype(f32).reshape(local, model_width)
+    scaled_two = grad_two * mlp_gain_full
+    grad_own = cotangent.astype(f32).reshape(local, model_width)
+    grad_residual = (
+        grad_own
+        + recip_two * scaled_two
+        - residual * recip_two**3 * jnp.mean(scaled_two * residual, -1, keepdims=True)
+    )
+    grad_branch = grad_residual.astype(bf16).reshape(inputs.shape)
+    branch_all = gather_ctx(grad_branch).reshape(tokens, model_width)
+
+    def reduce_dp(partial):
+        return lax.psum_scatter(partial.astype(bf16), "dp", scatter_dimension=0, tiled=True)
+
+    def back_exchange(rows):
+        return exchange(rows.reshape(ranks, weight_rows, -1)).astype(f32)
+
+    down_grad = reduce_dp(mm(hidden_low, grad_all, "nf,nd->fd")).astype(f32)
+    mlp_grad = back_exchange(reduce_dp(mm(normed_all, grad_both, "nd,nf->df")))
+
+    def hidden_rows(block):
+        split = block.reshape(ranks, weight_rows, dp_size, piece)
+        return split.transpose(1, 2, 0, 3).reshape(weight_rows, ff_width)
+
+    gate_grad = hidden_rows(mlp_grad[..., :hidden_width])
+    up_grad = hidden_rows(mlp_grad[..., hidden_width:])
+
+    grad_attended = mm(branch_all, out_weight, "nd,kd->nk").astype(bf16)
+    out_partial = reduce_dp(mm(attended, branch_all, "nk,nd->kd"))
+    output_grad = lax.ppermute(out_partial, ("dp", "ctx"), from_rank).astype(f32)
+    grad_heads = grad_attended.reshape(seq_here, seq_length, group, HEAD_DIM)
+    grad_probs = mm(grad_heads, values_low, "sqgd,skd->sgqk")
+    weighted = jnp.sum(probs * grad_probs, -1, keepdims=True)
+    grad_scores = (probs * (grad_probs - weighted)).astype(bf16)
+    grad_queries = mm(grad_scores, keys_rot, "sgqk,skd->sqgd").reshape(
+        seq_here, seq_length, group_width
+    )
+    grad_keys = mm(grad_scores, queries, "sgqk,sqgd->skd")
+    grad_values = mm(probs_low, grad_heads, "sgqk,sqgd->skd")
+    grad_q = rotate(grad_queries * score_scale, cosine, sine_table, HEAD_DIM, True)
+    grad_k = rotate(grad_keys, cosine, sine_table, HEAD_DIM, True)
+    grad_project = jnp.concatenate([grad_q, grad_k, grad_values], -1).astype(bf16)
+    grad_project = grad_project.reshape(tokens, head_width)
+    grad_one = mm(grad_project, head_weight, "nk,dk->nd").astype(bf16)
+    grad_one = reduce_ctx(grad_one.reshape(seq_here, seq_length, model_width))
+    grad_one = grad_one.astype(f32).reshape(local, model_width)
+    head_grad = back_exchange(reduce_dp(mm(normed_one, grad_project, "nd,nk->dk")))
+    recip_one = row_norm(own)
+    scaled_one = grad_one * attn_gain_full
+    inputs_grad = (
+        grad_residual
+        + recip_one * scaled_one
+        - own * recip_one**3 * jnp.mean(scaled_one * own, -1, keepdims=True)
+    ).astype(bf16)
+
+    def from_heads(block):
+        return block.transpose(1, 0, 2).reshape(weight_rows, -1)
+
+    query_grad = from_heads(head_grad[..., :group_width])
+    key_grad = from_heads(head_grad[..., group_width : group_width + HEAD_DIM])
+    value_grad = from_heads(head_grad[..., group_width + HEAD_DIM :])
+
+    def overlap(weight, grad):
+        return jnp.sum(weight.astype(f32) * grad, -1)
+
+    attn_gain_grad = (
+        overlap(query_weight, query_grad)
+        + overlap(key_weight, key_grad)
+        + overlap(value_weight, value_grad)
+    ) / attn_gain.astype(f32)
+    mlp_gain_grad = (overlap(gate_weight, gate_grad) + overlap(up_weight, up_grad)) / (
+        mlp_gain.astype(f32)
+    )
+    return (
+        layer_out.reshape(inputs.shape),
+        inputs_grad.reshape(inputs.shape),
+        query_grad,
+        key_grad,
+        value_grad,
+        output_grad,
+        attn_gain_grad,
+        gate_grad,
+        up_grad,
+        down_grad,
+        mlp_gain_grad,
+    )
+
+
 def solution(mesh):
     placed = (
         P("dp", "ctx", None),
@@ -341,8 +558,10 @@
         P(("dp", "ctx"), None),
         P(("dp", "ctx")),
     )
+    dp_size, ctx_size = mesh.shape["dp"], mesh.shape["ctx"]
+    chosen = functools.partial(head_body, dp_size) if ctx_size == KV_HEADS else body
     return jax.shard_map(
-        body,
+        chosen,
         mesh=mesh,
         in_specs=placed,
         out_specs=(

time: 1850 us -> 662 us (0.36)
  waiting for transfers between devices: 1390 us -> 383 us
  matrix products: 191 us -> 66.5 us
  local copies, waits for them, and re-layouts: 109 us -> 18.3 us
  blocking collectives: 42.1 us -> 127 us
  other arithmetic: 69.3 us -> 30.8 us
  loops' own time: 22.2 us -> 0 us
    reduce_scatter x3 -> x8, waiting for transfers between devices: 946 us -> 212 us  [the longest x4 125 us: reduce_ctx(): return lax.psum_scatter(partial, 'ctx', scatter_dimension=1, tiled=True)]
    all_gather x8 -> x7, waiting for transfers between devices: 426 us -> 169 us  [the longest x4 102 us: gather_ctx(): return lax.all_gather(block, 'ctx', axis=1, tiled=True)]
    dot_general x74 -> x18, matrix products: 191 us -> 66.5 us  [mm(): return jnp.einsum(dims, left, right, preferred_element_type=jnp.float32)]
    all_gather x0 -> x2, blocking collectives: none -> 67.4 us  [the longest x1 57.5 us: head_body(): lax.all_gather(jnp.stack([attn_gain, mlp_gain]), ('dp', 'ctx'), axis=1, t...]
    all_to_all x0 -> x2, blocking collectives: none -> 59.4 us  [exchange(): lax.all_to_all(packed, 'ctx', split_axis=0, concat_axis=0, tiled=True)]
    concatenate x3 -> x1, other arithmetic: 53.2 us -> 1.21 us  [head_body(): jnp.concatenate([hidden_columns(gate_weight), hidden_columns(up_weight)],...]
    unnamed x1 -> x0, blocking collectives: 42.1 us -> none
    dynamic_slice x32 -> x0, local copies, waits for them, and re-layouts: 25.6 us -> none  [the longest x16 16.2 us: group_slice(): lax.dynamic_slice_in_dim(source, kv_head * group_width, group_width, 2)]
  transfers between devices with their start and end apart: 12 -> 19, of which waited for: 12 -> 13; matrix products, arithmetic and copies ran while one was open for 12% -> 13% of each run, Pallas kernels for 0% -> 0%
where the time goes in v1:
time: 662 us; the launch traced here: 653 us
  waiting for transfers between devices  383 us (58%)
  blocking collectives  127 us (19%)
  matrix products  66.5 us (10%)
  other arithmetic  30.8 us (5%)
  local copies, waits for them, and re-layouts  18.3 us (3%)
  between operations  15.1 us (2%)
  starting transfers between devices  12.7 us (2%)
    reduce_scatter x4, waiting for transfers between devices, reduce_ctx(): return lax.psum_scatter(partial, 'ctx', scatter_dimension=1, tiled=True)  125 us
    all_gather x4, waiting for transfers between devices, gather_ctx(): return lax.all_gather(block, 'ctx', axis=1, tiled=True)  102 us
    reduce_scatter x4, waiting for transfers between devices, reduce_dp(): lax.psum_scatter(partial.astype(bf16), 'dp', scatter_dimension=0, tiled=T...  86.1 us
    dot_general x18, matrix products, mm(): return jnp.einsum(dims, left, right, preferred_element_type=jnp.float32)  66.5 us
    all_to_all x2, blocking collectives, exchange(): lax.all_to_all(packed, 'ctx', split_axis=0, concat_axis=0, tiled=True)  59.4 us
    all_gather x1, blocking collectives, head_body(): lax.all_gather(jnp.stack([attn_gain, mlp_gain]), ('dp', 'ctx'), axis=1, t...  57.5 us
    all_gather x1, waiting for transfers between devices, head_body(): mlp_weight = lax.all_gather(mlp_mine, 'dp', axis=0, tiled=True)  44.1 us
    all_gather x1, waiting for transfers between devices, head_body(): down_full = lax.all_gather(down_weight, 'dp', axis=0, tiled=True)  23.1 us
  transfers between devices with their start and end apart: 19, of which 13 were waited for; matrix products, arithmetic and copies ran while one was open for 13% of the time, Pallas kernels for 0%

profile of v1, /device:TPU:0, one launch (start us, length us, event | category | flops | bytes accessed | tf_op | source)
XLA Modules:
  0.0 653.4 jit_solution(1039694719089228536)
XLA Ops:
  11.4 21.9 %all_to_all.20 = bf16[8,48,384]{2,1,0:T(8,128)(2,1)S(1)} all-to-all(bf16[8,48,384]{2,1,0:T(8,128)(2,1)S(1)} %copy.76), channel_id=1, replica_groups=mesh['dp'=4,'ctx'=8] {'ctx'}, dimensions={0} | all-to-all | bytes 589824 | tf_op jit(solution)/shard_map/all_to_all | solution.py:385
  34.9 57.5 %all-gather = bf16[32,48,2]{1,2,0:T(2,128)(2,1)S(1)} all-gather(bf16[1,48,2]{1,2,0:T(2,128)(2,1)S(1)} %maximum_bitcast_fusion.4), channel_id=1, replica_groups=mesh['dp'=4,'ctx'=8] {'dp','ctx'}, dimensions={0}, use_global_device_ids=true | all-gather | bytes 6336 | tf_op jit(solution)/shard_map/all_gather | solution.py:406
  93.2 9.9 %all_gather.30 = bf16[192,1536]{1,0:T(8,128)(2,1)S(1)} all-gather(bf16[48,1536]{1,0:T(8,128)(2,1)S(1)} %collective-permute-done), channel_id=1, replica_groups=mesh['dp'=4,'ctx'=8] {'dp'}, dimensions={0}, use_global_device_ids=true | all-gather | bytes 737280 | tf_op jit(solution)/shard_map/all_gather | solution.py:401
  103.0 2.6 multiply_reduce_fusion
  105.7 3.7 fusion.6
  113.1 2.7 convolution_convert_fusion
  120.2 37.5 %all_to_all.21 = bf16[8,48,1024]{2,1,0:T(8,128)(2,1)} all-to-all(bf16[8,48,1024]{2,1,0:T(8,128)(2,1)S(1)} %pad_maximum_fusion.3), channel_id=1, replica_groups=mesh['dp'=4,'ctx'=8] {'ctx'}, dimensions={0} | all-to-all | bytes 1572864 | tf_op jit(solution)/shard_map/all_to_all | solution.py:385
  157.8 8.7 %reduce-scatter.9.cloned.1.call-done = bf16[2,64,1536]{2,1,0:T(8,128)(2,1)} async-done(((bf16[2,512,1536]{2,1,0:T(8,128)(2,1)}), bf16[2,64,1536]{2,1,0:T(8,128)(2,1)}) %reduce-scatter.9.cloned.1.call-update) | async-done | bytes 393232 | tf_op jit(solution)/shard_map/reduce_scatter | solution.py:341
  167.7 1.9 multiply_convert_fusion.5
  171.2 44.1 %all-gather.15.cloned.1.call-done = bf16[1536,1024]{1,0:T(8,128)(2,1)} async-done(((bf16[384,1024]{1,0:T(8,128)(2,1)}), bf16[1536,1024]{1,0:T(8,128)(2,1)}) %all-gather.15.cloned.1.call-update) | async-done | bytes 3145744 | tf_op jit(solution)/shard_map/all_gather | solution.py:404
  215.3 40.3 %all-gather.13.cloned.1.call-done = bf16[2,512,1536]{2,1,0:T(8,128)(2,1)} async-done(((bf16[2,64,1536]{2,1,0:T(8,128)(2,1)}), bf16[2,512,1536]{2,1,0:T(8,128)(2,1)}) %all-gather.13.cloned.1.call-update) | async-done | bytes 3145744 | tf_op jit(solution)/shard_map/all_gather | solution.py:337
  255.5 8.3 %fusion.49 = f32[1024,1024]{0,1:T(8,128)} fusion(bf16[1024,1536]{1,0:T(8,128)(2,1)} %bitcast.199, bf16[1536,1024]{1,0:T(8,128)(2,1)} %all-gather.15.cloned.1.call-done), kind=kOutput, calls=%fused_computation.129 | convolution fusion | flops 3221225472 | bytes 10485760 | tf_op jit(solution)/shard_map/nd,df->nf/dot_general | solution.py:345
  263.9 23.1 %all-gather.17.cloned.1.call-done = bf16[512,1536]{1,0:T(8,128)(2,1)} async-done(((bf16[128,1536]{1,0:T(8,128)(2,1)}), bf16[512,1536]{1,0:T(8,128)(2,1)}) %all-gather.17.cloned.1.call-update) | async-done | bytes 1572880 | tf_op jit(solution)/shard_map/all_gather | solution.py:405
  287.0 39.8 %all-gather.19.cloned.1.call-done = bf16[2,512,1536]{2,1,0:T(8,128)(2,1)} async-done(((bf16[2,64,1536]{2,1,0:T(8,128)(2,1)}), bf16[2,512,1536]{2,1,0:T(8,128)(2,1)}) %all-gather.19.cloned.1.call-update) | async-done | bytes 3145744 | tf_op jit(solution)/shard_map/all_gather | solution.py:337
  326.8 7.2 %multiply_convert_fusion.3 = (bf16[1024,512]{0,1:T(8,128)(2,1)S(1)}, bf16[1024,512]{0,1:T(8,128)(2,1)S(1)}, bf16[1024,512]{0,1:T(8,128)(2,1)}) fusion(f32[1024,1024]{0,1:T(8,128)} %fusion.49, bf16[1024,1536]{1,0:T(8,128)(2,1)} %bitcast.197, bf16[512,1536]{1,0:T(8,128)(2,1)} %all-gather.17.cloned.1.call-done), kind=kOutput, calls=%fused_computation.29 | convolution fusion | flops 1618477056 | bytes 12058624 | tf_op jit(solution)/shard_map/nd,fd->nf/dot_general | solution.py:345
  334.1 5.0 convolution_convert_fusion.4
  339.1 39.4 %reduce-scatter.13.cloned.1.call-done = bf16[2,64,1536]{2,1,0:T(8,128)(2,1)} async-done(((bf16[2,512,1536]{2,1,0:T(8,128)(2,1)}), bf16[2,64,1536]{2,1,0:T(8,128)(2,1)}) %reduce-scatter.13.cloned.1.call-update) | async-done | bytes 393232 | tf_op jit(solution)/shard_map/reduce_scatter | solution.py:341
  378.5 1.3 fusion.17
  379.9 2.1 fusion.26
  382.0 7.6 %convolution_convert_fusion.3 = bf16[1536,1024]{1,0:T(8,128)(2,1)} fusion(bf16[1024,1536]{1,0:T(8,128)(2,1)} %bitcast.200, bf16[1024,512]{0,1:T(8,128)(2,1)} %copy-done.38, bf16[1024,512]{0,1:T(8,128)(2,1)} %copy-done.37), kind=kOutput, calls=%fused_computation.16 | convolution fusion | flops 3226992640 | bytes 8388608 | tf_op jit(solution)/shard_map/nd,nf->df/dot_general | solution.py:345
  390.0 4.5 fusion.1
  394.4 3.0 convolution_convert_fusion.5
  397.5 22.2 %all-gather.21.cloned.1.call-done = bf16[2,512,1536]{2,1,0:T(8,128)(2,1)} async-done(((bf16[2,64,1536]{2,1,0:T(8,128)(2,1)}), bf16[2,512,1536]{2,1,0:T(8,128)(2,1)}) %all-gather.21.cloned.1.call-update) | async-done | bytes 3145744 | tf_op jit(solution)/shard_map/all_gather | solution.py:337
  419.7 3.8 convolution_convert_fusion.8
  423.5 1.3 reshape.388
  424.8 3.4 fusion.16
  428.5 2.4 fusion.2
  430.9 1.3 fusion.4
  435.6 2.9 convolution_convert_fusion.6
  438.6 3.6 convolution_convert_fusion.7
  442.6 4.7 convolution_convert_fusion.1
  447.4 1.4 copy-done.34
  448.7 4.8 convolution_convert_fusion.2
  453.6 11.8 %reduce-scatter.21.cloned.1.call-done = bf16[384,1024]{1,0:T(8,128)(2,1)} async-done(((bf16[1536,1024]{1,0:T(8,128)(2,1)}), bf16[384,1024]{1,0:T(8,128)(2,1)}) %reduce-scatter.21.cloned.1.call-update) | async-done | bytes 786448 | tf_op jit(solution)/shard_map/reduce_scatter | solution.py:471
  465.3 4.6 all-to-all-start.3
  469.9 29.6 %reduce-scatter.23.cloned.1.call-done = bf16[128,1536]{1,0:T(8,128)(2,1)} async-done(((bf16[512,1536]{1,0:T(8,128)(2,1)}), bf16[128,1536]{1,0:T(8,128)(2,1)}) %reduce-scatter.23.cloned.1.call-update) | async-done | bytes 393232 | tf_op jit(solution)/shard_map/reduce_scatter | solution.py:471
  499.5 2.0 convert_element_type.215
  503.9 1.4 reshape.397
  505.3 1.3 copy.93
  506.6 24.4 %reduce-scatter.17.cloned.1.call-done = bf16[384,384]{1,0:T(8,128)(2,1)} async-done(((bf16[1536,384]{1,0:T(8,128)(2,1)}), bf16[384,384]{1,0:T(8,128)(2,1)}) %reduce-scatter.17.cloned.1.call-update) | async-done | bytes 294928 | tf_op jit(solution)/shard_map/reduce_scatter | solution.py:471
  531.0 4.6 all-to-all-start.2
  535.7 3.3 multiply_reduce_fusion.1
  539.0 20.4 %reduce-scatter.19.cloned.1.call-done = bf16[48,1536]{1,0:T(8,128)(2,1)} async-done(((bf16[192,1536]{1,0:T(8,128)(2,1)}), bf16[48,1536]{1,0:T(8,128)(2,1)}) %reduce-scatter.19.cloned.1.call-update) | async-done | bytes 147472 | tf_op jit(solution)/shard_map/reduce_scatter | solution.py:471
  559.3 1.6 collective-permute-start.1
  565.1 37.2 %reduce-scatter.15.cloned.1.call-done = bf16[2,64,1536]{2,1,0:T(8,128)(2,1)} async-done(((bf16[2,512,1536]{2,1,0:T(8,128)(2,1)}), bf16[2,64,1536]{2,1,0:T(8,128)(2,1)}) %reduce-scatter.15.cloned.1.call-update) | async-done | bytes 393232 | tf_op jit(solution)/shard_map/reduce_scatter | solution.py:341
  602.2 1.2 fusion.21
  603.5 40.2 %reduce-scatter.11.cloned.1.call-done = bf16[2,64,1536]{2,1,0:T(8,128)(2,1)} async-done(((bf16[2,512,1536]{2,1,0:T(8,128)(2,1)}), bf16[2,64,1536]{2,1,0:T(8,128)(2,1)}) %reduce-scatter.11.cloned.1.call-update) | async-done | bytes 393232 | tf_op jit(solution)/shard_map/reduce_scatter | solution.py:341
  643.7 2.7 fusion.20
  (183 shorter events, 28.3 us)
Async XLA Ops:
  7.2 27.0 %copy-start.35 = (bf16[48,1536]{1,0:T(8,128)(2,1)S(1)}, bf16[48,1536]{1,0:T(8,128)(2,1)}, u32[]{:S(2)}) copy-start(bf16[48,1536]{1,0:T(8,128)(2,1)} %param.16) | copy-start | bytes 442372
  7.2 27.7 %copy-start.28 = (bf16[48]{0:T(256)(128)(2,1)S(1)}, bf16[48]{0:T(256)(128)(2,1)}, u32[]{:S(2)}) copy-start(bf16[48]{0:T(256)(128)(2,1)} %param.17) | copy-start | bytes 292
  7.2 27.7 %copy-start.30 = (bf16[48]{0:T(256)(128)(2,1)S(1)}, bf16[48]{0:T(256)(128)(2,1)}, u32[]{:S(2)}) copy-start(bf16[48]{0:T(256)(128)(2,1)} %param.21) | copy-start | bytes 292
  7.2 95.8 %all-gather.9.cloned.1.call-start = ((), (), s32[]{:S(2)}) async-start(), calls=%async_computation.12 | async-start | bytes 3538944 | tf_op jit(solution)/shard_map/all_gather | solution.py:337
  7.9 97.7 %all-gather.11.cloned.1.call-start = ((), (), s32[]{:S(2)}) async-start(), calls=%async_computation.13 | async-start | bytes 1474560 | tf_op jit(solution)/shard_map/all_gather | solution.py:396
  34.1 132.3 %reduce-scatter.9.cloned.1.call-start = ((), (), s32[]{:S(2)}) async-start(), calls=%async_computation.14 | async-start | bytes 3538944 | tf_op jit(solution)/shard_map/reduce_scatter | solution.py:341
  34.2 58.9 %collective-permute-start = (bf16[48,1536]{1,0:T(8,128)(2,1)S(1)}, bf16[48,1536]{1,0:T(8,128)(2,1)S(1)}, u32[]{:S(2)}, u32[]{:S(2)}) collective-permute-start(bf16[48,1536]{1,0:T(8,128)(2,1)S(1)} %copy-done.35), channel_id=1, source_target_pairs={{0,0},{1,8},{2,16},{3,24},{4,1},{5,9},{6,17},{7,25},{8,2},{9,10},{... | collective-permute-start | bytes 442376 | tf_op jit(solution)/shard_map/ppermute | solution.py:400
  115.7 99.5 %all-gather.15.cloned.1.call-start = ((), (), s32[]{:S(2)}) async-start(), calls=%async_computation.16 | async-start | bytes 3932160 | tf_op jit(solution)/shard_map/all_gather | solution.py:404
  117.8 48.6 %copy-start.2 = (bf16[2,64,1536]{2,1,0:T(8,128)(2,1)S(1)}, bf16[2,64,1536]{2,1,0:T(8,128)(2,1)}, u32[]{:S(2)}) copy-start(bf16[2,64,1536]{2,1,0:T(8,128)(2,1)} %param.11) | copy-start | bytes 1179652
  157.7 97.8 %all-gather.13.cloned.1.call-start = ((), (), s32[]{:S(2)}) async-start(), calls=%async_computation.15 | async-start | bytes 3538944 | tf_op jit(solution)/shard_map/all_gather | solution.py:337
  167.7 212.1 %copy-start.20 = (f32[2,64]{1,0:T(2,128)}, f32[2,64]{1,0:T(2,128)S(1)}, u32[]{:S(2)}) copy-start(f32[2,64]{1,0:T(2,128)S(1)} %get-tuple-element.43) | copy-start | bytes 1540
  167.7 212.1 %copy-start.22 = (f32[2,64]{1,0:T(2,128)}, f32[2,64]{1,0:T(2,128)S(1)}, u32[]{:S(2)}) copy-start(f32[2,64]{1,0:T(2,128)S(1)} %get-tuple-element.42) | copy-start | bytes 1540
  169.6 117.3 %all-gather.17.cloned.1.call-start = ((), (), s32[]{:S(2)}) async-start(), calls=%async_computation.17 | async-start | bytes 1966080 | tf_op jit(solution)/shard_map/all_gather | solution.py:405
  170.2 156.6 %all-gather.19.cloned.1.call-start = ((), (), s32[]{:S(2)}) async-start(), calls=%async_computation.19 | async-start | bytes 3538944 | tf_op jit(solution)/shard_map/all_gather | solution.py:337
  171.0 207.6 %reduce-scatter.13.cloned.1.call-start = ((), (), s32[]{:S(2)}) async-start(), calls=%async_computation.20 | async-start | bytes 3538944 | tf_op jit(solution)/shard_map/reduce_scatter | solution.py:341
  326.8 7.2 %copy-start.33 = (bf16[1536,1024]{1,0:T(8,128)(2,1)S(1)}, bf16[1536,1024]{1,0:T(8,128)(2,1)}, u32[]{:S(2)}) copy-start(bf16[1536,1024]{1,0:T(8,128)(2,1)} %all-gather.15.cloned.1.call-done) | copy-start | bytes 9437188
  334.1 5.0 copy-start.37
  334.1 5.0 copy-start.38
  339.1 39.5 %copy-start.3 = (bf16[2,64,1536]{2,1,0:T(8,128)(2,1)S(1)}, bf16[2,64,1536]{2,1,0:T(8,128)(2,1)}, u32[]{:S(2)}) copy-start(bf16[2,64,1536]{2,1,0:T(8,128)(2,1)} %reduce-scatter.9.cloned.1.call-done) | copy-start | bytes 1179652
  339.1 40.8 %copy-start.4 = (bf16[2,64,1536]{2,1,0:T(8,128)(2,1)S(1)}, bf16[2,64,1536]{2,1,0:T(8,128)(2,1)}, u32[]{:S(2)}) copy-start(bf16[2,64,1536]{2,1,0:T(8,128)(2,1)} %param.12) | copy-start | bytes 1179652
  339.1 80.6 %all-gather.21.cloned.1.call-start = ((), (), s32[]{:S(2)}) async-start(), calls=%async_computation.21 | async-start | bytes 3538944 | tf_op jit(solution)/shard_map/all_gather | solution.py:337
  379.8 9.8 %copy-start.24 = (f32[2,64]{1,0:T(2,128)}, f32[2,64]{1,0:T(2,128)S(1)}, u32[]{:S(2)}) copy-start(f32[2,64]{1,0:T(2,128)S(1)} %broadcast_multiply_fusion.1) | copy-start | bytes 1540
  382.0 83.3 %reduce-scatter.21.cloned.1.call-start = ((), (), s32[]{:S(2)}) async-start(), calls=%async_computation.25 | async-start | bytes 3932160 | tf_op jit(solution)/shard_map/reduce_scatter | solution.py:471
  389.7 109.8 %reduce-scatter.23.cloned.1.call-start = ((), (), s32[]{:S(2)}) async-start(), calls=%async_computation.26 | async-start | bytes 1966080 | tf_op jit(solution)/shard_map/reduce_scatter | solution.py:471
  390.0 4.5 copy-start.32
  390.0 4.5 copy-start.36
  397.4 133.6 %reduce-scatter.17.cloned.1.call-start = ((), (), s32[]{:S(2)}) async-start(), calls=%async_computation.23 | async-start | bytes 1474560 | tf_op jit(solution)/shard_map/reduce_scatter | solution.py:471
  424.8 3.7 copy-start.1
  438.6 120.8 %reduce-scatter.19.cloned.1.call-start = ((), (), s32[]{:S(2)}) async-start(), calls=%async_computation.24 | async-start | bytes 737280 | tf_op jit(solution)/shard_map/reduce_scatter | solution.py:471
  442.2 160.0 %reduce-scatter.15.cloned.1.call-start = ((), (), s32[]{:S(2)}) async-start(), calls=%async_computation.22 | async-start | bytes 3538944 | tf_op jit(solution)/shard_map/reduce_scatter | solution.py:341
  447.3 196.4 %reduce-scatter.11.cloned.1.call-start = ((), (), s32[]{:S(2)}) async-start(), calls=%async_computation.18 | async-start | bytes 3538944 | tf_op jit(solution)/shard_map/reduce_scatter | solution.py:341
  465.3 36.7 %all-to-all-start.3 = ((bf16[8,48,1024]{2,1,0:T(8,128)(2,1)}), bf16[8,48,1024]{2,1,0:T(8,128)(2,1)S(1)}, u32[]{:S(2)}, u32[]{:S(2)}) async-start(bf16[8,48,1024]{2,1,0:T(8,128)(2,1)} %bitcast.188), calls=%async_computation.10 | async-start | bytes 1572864 | tf_op jit(solution)/shard_map/all_to_all | solution.py:385
  503.1 32.5 %copy-start.9 = (bf16[48,4096]{1,0:T(8,128)(2,1)S(1)}, bf16[48,4096]{1,0:T(8,128)(2,1)}, u32[]{:S(2)}) copy-start(bf16[48,4096]{1,0:T(8,128)(2,1)} %param.19) | copy-start | bytes 1179652
  503.1 32.5 %copy-start.11 = (bf16[48,4096]{1,0:T(8,128)(2,1)S(1)}, bf16[48,4096]{1,0:T(8,128)(2,1)}, u32[]{:S(2)}) copy-start(bf16[48,4096]{1,0:T(8,128)(2,1)} %param.18) | copy-start | bytes 1179652
  506.6 54.3 %copy-start.31 = (bf16[48]{0:T(256)(128)(2,1)S(1)}, bf16[48]{0:T(256)(128)(2,1)}, u32[]{:S(2)}) copy-start(bf16[48]{0:T(256)(128)(2,1)} %param.21) | copy-start | bytes 292
  531.0 31.1 %all-to-all-start.2 = ((bf16[8,48,384]{2,1,0:T(8,128)(2,1)}), bf16[8,48,384]{2,1,0:T(8,128)(2,1)}, u32[]{:S(2)}, u32[]{:S(2)}) async-start(bf16[8,48,384]{2,1,0:T(8,128)(2,1)} %bitcast.192), calls=%async_computation.7 | async-start | bytes 589824 | tf_op jit(solution)/shard_map/all_to_all | solution.py:385
  539.0 25.3 %copy-start.17 = (bf16[48,1536]{1,0:T(8,128)(2,1)S(1)}, bf16[48,1536]{1,0:T(8,128)(2,1)}, u32[]{:S(2)}) copy-start(bf16[48,1536]{1,0:T(8,128)(2,1)} %param.13) | copy-start | bytes 442372
  559.3 2.1 collective-permute-start.1
  561.4 3.0 copy-start.19
  563.2 80.5 %copy-start.5 = (bf16[2,64,1536]{2,1,0:T(8,128)(2,1)S(1)}, bf16[2,64,1536]{2,1,0:T(8,128)(2,1)}, u32[]{:S(2)}) copy-start(bf16[2,64,1536]{2,1,0:T(8,128)(2,1)} %reduce-scatter.13.cloned.1.call-done) | copy-start | bytes 1179652
  563.2 80.5 %copy-start.21 = (f32[2,64]{1,0:T(2,128)S(1)}, f32[2,64]{1,0:T(2,128)}, u32[]{:S(2)}) copy-start(f32[2,64]{1,0:T(2,128)} %copy-done.20) | copy-start | bytes 1540
  563.2 80.5 %copy-start.23 = (f32[2,64]{1,0:T(2,128)S(1)}, f32[2,64]{1,0:T(2,128)}, u32[]{:S(2)}) copy-start(f32[2,64]{1,0:T(2,128)} %copy-done.22) | copy-start | bytes 1540
  563.2 80.5 %copy-start.25 = (f32[2,64]{1,0:T(2,128)S(1)}, f32[2,64]{1,0:T(2,128)}, u32[]{:S(2)}) copy-start(f32[2,64]{1,0:T(2,128)} %copy-done.24) | copy-start | bytes 1540
  563.2 80.5 %copy-start.26 = (f32[2,64]{1,0:T(2,128)S(1)}, f32[2,64]{1,0:T(2,128)}, u32[]{:S(2)}) copy-start(f32[2,64]{1,0:T(2,128)} %get-tuple-element.40) | copy-start | bytes 1540
  563.2 80.5 %copy-start.27 = (f32[2,64]{1,0:T(2,128)S(1)}, f32[2,64]{1,0:T(2,128)}, u32[]{:S(2)}) copy-start(f32[2,64]{1,0:T(2,128)} %get-tuple-element.41) | copy-start | bytes 1540
  563.6 82.8 %copy-start.15 = (f32[48,768]{1,0:T(8,128)}, f32[48,768]{1,0:T(8,128)S(1)}, u32[]{:S(2)}) copy-start(f32[48,768]{1,0:T(8,128)S(1)} %reshape.395) | copy-start | bytes 442372
  564.0 82.4 %copy-start.12 = (f32[48,1536]{1,0:T(8,128)}, f32[48,1536]{1,0:T(8,128)S(1)}, u32[]{:S(2)}) copy-start(f32[48,1536]{1,0:T(8,128)S(1)} %reshape.393) | copy-start | bytes 884740
  564.2 82.1 %copy-start.16 = (f32[48,768]{1,0:T(8,128)}, f32[48,768]{1,0:T(8,128)S(1)}, u32[]{:S(2)}) copy-start(f32[48,768]{1,0:T(8,128)S(1)} %reshape.394) | copy-start | bytes 442372
  (10 other events, 18.0 us)
Sparse Core Ops, SparseCore 0:
  9.6 52.2 all-gather.8
  64.3 27.4 all-gather.10
  115.9 50.5 reduce-scatter.8
  168.2 47.0 all-gather.14
  217.3 38.1 all-gather.12
  257.2 29.7 all-gather.16
  288.6 38.1 all-gather.18
  339.2 39.2 reduce-scatter.12
  382.1 37.4 all-gather.20
  422.5 42.8 reduce-scatter.20
  468.3 31.1 reduce-scatter.22
  502.3 28.7 reduce-scatter.16
  533.9 25.3 reduce-scatter.18
  561.5 40.6 reduce-scatter.14
  604.4 39.2 reduce-scatter.10
